TPU v7x, 256 devices: a whole 4x4x8 slice. The times are simulated.
256 devices in a mesh: ctx: 32 (over z, x_lo, core), mp: 8 (over y, x_hi).
Axes of the slice: x: 4 (x_hi: 2, x_lo: 2; x = x_hi * 2 + x_lo), y: 4, z: 8, core: 2. Of those that a mesh axis runs over, the one named last changes fastest.
Arguments:
- byte_qkv: bfloat16 [16384, 3, 4096], P('ctx', None, 'mp'), may hold values from -14 to 14
- kv_weight: bfloat16 [4096, 2, 4096], P(None, None, 'mp'), may hold values from -4 to 4
- patch_bounds: int32 [32, 161], replicated, may hold values from 0 to 16384, as said below
Outputs:
- mixed: bfloat16 [5120, 4096], P('ctx', 'mp')
Inputs may be any that keep to these rules, and one draw needn't show every extreme that they name: `patch_bounds`: row c lists in increasing order the first bytes of the patches that begin in bytes c * 512 to (c + 1) * 512 - 1, then the end of its last patch, repeated to the end of the row. The patches cover all 16384 bytes, each is 1 to 16 bytes long, one is exactly 16 long, and some row lists exactly 160 patches.
All inputs are finite; a program needn't handle non-finite values.
Results may differ from a plain program's by a relative error of at most 0.002.
The roundings to bfloat16 on the way count: a program that leaves them out, or rounds other values in their place, can miss the bound.
Values may be sent and summed in bfloat16 or wider, within the bound.
A program may use at most 128 MiB of HBM per device.

v0:
```python
import math
import jax
import jax.numpy as jnp
from jax import lax
from jax.sharding import PartitionSpec as P

D = 4096
HEADS = 32
WIN = 16
masked_score = -1e30


def passed_along(value, axis, steps):
    count = lax.axis_size(axis)
    initial, last = (max(0, -steps), min(count, count - steps))
    return lax.ppermute(value, axis, [(source, source + steps) for source in range(initial, last)])


def shards(byte_qkv, kv_weight, patch_bounds):
    byte_rows = byte_qkv.shape[0]
    col_width = byte_qkv.shape[2]
    head_dim = D // HEADS
    heads_here = col_width // head_dim
    slot_count = patch_bounds.shape[1] - 1
    score_scale = 1.0 / math.sqrt(head_dim)
    ctx_place = lax.axis_index("ctx")
    my_bounds = lax.dynamic_index_in_dim(patch_bounds, ctx_place, 0, keepdims=False)
    starts = my_bounds[:slot_count]
    lengths = my_bounds[1:] - starts
    live_slot = lengths > 0
    edge_rows = passed_along(byte_qkv[:WIN], "ctx", -1)
    extended = jnp.concatenate([byte_qkv, edge_rows], axis=0)
    offsets = jnp.arange(WIN, dtype=jnp.int32)
    local_start = jnp.clip(starts - ctx_place * byte_rows, 0, byte_rows)
    window = extended[local_start[:, None] + offsets[None, :]]
    window = window.reshape(slot_count, WIN, 3, heads_here, head_dim)
    inside = offsets[None, :] < lengths[:, None]
    queries = jnp.max(jnp.where(inside[:, :, None, None], window[:, :, 0], -jnp.inf), axis=1)
    queries = jnp.where(live_slot[:, None, None], queries, 0)
    scores = (
        jnp.einsum("shd,swhd->shw", queries, window[:, :, 1], preferred_element_type=jnp.float32)
        * score_scale
    )
    scores = jnp.where(inside[:, None, :], scores, masked_score)
    scores = scores - jnp.max(scores, axis=2, keepdims=True)
    exp_terms = jnp.exp(scores)
    weights = (exp_terms / jnp.sum(exp_terms, axis=2, keepdims=True)).astype(jnp.bfloat16)
    pooled = jnp.einsum(
        "shw,swhd->shd", weights, window[:, :, 2], preferred_element_type=jnp.float32
    )
    patch_state = (
        jnp.where(live_slot[:, None, None], pooled, 0.0)
        .astype(jnp.bfloat16)
        .reshape(slot_count, col_width)
    )
    flat_weight = kv_weight.reshape(kv_weight.shape[0], 2 * col_width)
    projected = jnp.dot(
        lax.all_gather(patch_state, "mp", axis=1, tiled=True),
        flat_weight,
        preferred_element_type=jnp.float32,
    )
    key_value = projected.astype(jnp.bfloat16)
    query_heads = patch_state.reshape(slot_count, heads_here, head_dim)
    query_slot = ctx_place * slot_count + jnp.arange(slot_count, dtype=jnp.int32)
    valid_all = (patch_bounds[:, 1:] > patch_bounds[:, :-1]).reshape(-1)
    shard_piece = lax.all_gather(key_value, "ctx", axis=0, tiled=True)
    top_score = jnp.full((heads_here, slot_count), masked_score, jnp.float32)
    piece_rows = shard_piece.shape[0]
    key_part = shard_piece[:, :col_width].reshape(piece_rows, heads_here, head_dim)
    value_part = shard_piece[:, col_width:].reshape(piece_rows, heads_here, head_dim)
    key_slot = jnp.arange(piece_rows, dtype=jnp.int32)
    visible = (key_slot[None, :] <= query_slot[:, None]) & valid_all[None, :]
    global_scores = (
        jnp.einsum("qhd,khd->hqk", query_heads, key_part, preferred_element_type=jnp.float32)
        * score_scale
    )
    global_scores = jnp.where(visible[None], global_scores, masked_score)
    new_top = jnp.maximum(top_score, jnp.max(global_scores, axis=2))
    exp_part = jnp.where(visible[None], jnp.exp(global_scores - new_top[:, :, None]), 0.0)
    denom_sum = jnp.sum(exp_part, axis=2)
    weighted = jnp.einsum(
        "hqk,khd->hqd", exp_part, value_part.astype(jnp.float32), precision=lax.Precision.HIGHEST
    )
    fold_state = (new_top, denom_sum, weighted)
    top_score, denom_sum, weighted = fold_state
    safe_total = jnp.where(denom_sum > 0, denom_sum, 1.0)
    attended = (weighted / safe_total[:, :, None]).transpose(1, 0, 2).reshape(slot_count, col_width)
    attended = jnp.where(live_slot[:, None], attended, 0.0)
    return (patch_state.astype(jnp.float32) + attended).astype(jnp.bfloat16)


def solution(mesh):
    return jax.shard_map(
        shards,
        mesh=mesh,
        in_specs=(P("ctx", None, "mp"), P(None, None, "mp"), P()),
        out_specs=P("ctx", "mp"),
        check_vma=False,
    )
```

profile of v0, /device:TPU:1, one launch (start us, length us, event | category | flops | bytes accessed | tf_op | source)
XLA Modules:
  0.0 252.5 jit_solution(9994078554285454188)
XLA Ops:
  6.5 2.8 %copy.29 = bf16[512,3,512]{2,1,0:T(4,128)(2,1)S(1)} copy(bf16[512,3,512]{2,0,1:T(8,128)(2,1)} %param.3) | data formatting | bytes 3145728 | tf_op args[0]
  9.3 1.3 copy-done
  10.7 5.1 %collective-permute-start = (bf16[16,3,512]{2,1,0:T(4,128)(2,1)S(1)}, bf16[16,3,512]{2,1,0:T(4,128)(2,1)S(1)}, u32[]{:S(2)}, u32[]{:S(2)}) collective-permute-start(bf16[16,3,512]{2,1,0:T(4,128)(2,1)S(1)} %slice.44), channel_id=1, source_target_pairs={{8,0},{16,8},{24,16},{32,24},{40,32},{48,40},{56,48},{64,56},{72,6... | collective-permute-start | bytes 147464 | tf_op jit(solution)/shard_map/ppermute | solution.py:16
  15.8 0.9 dynamic-slice_subtract_fusion
  16.7 0.1 iota_compare_fusion.1
  16.8 0.1 compare_select_fusion
  16.9 0.1 reshape.193
  17.0 0.1 collective-permute-done
  17.1 3.0 %pad_maximum_fusion = bf16[528,3,512]{2,1,0:T(4,128)(2,1)S(1)} fusion(bf16[16,3,512]{2,1,0:T(4,128)(2,1)S(1)} %collective-permute-done, bf16[512,3,512]{2,1,0:T(4,128)(2,1)} %copy-done), kind=kLoop, calls=%fused_computation.31 | loop fusion | flops 811008 | bytes 3244032 | tf_op jit(solution)/shard_map/concatenate | solution.py:32
  20.1 12.8 %gather_fusion = bf16[2560,3,512]{2,1,0:T(4,128)(2,1)} fusion(bf16[528,3,512]{2,1,0:T(4,128)(2,1)S(1)} %pad_maximum_fusion, s32[3072]{0:T(1024)S(1)} %pad_clamp_fusion), kind=kCustom, calls=%fused_computation | custom fusion | bytes 15738880 | tf_op jit(solution)/shard_map/gather | solution.py:35
  33.0 21.7 %reshape.205 = bf16[160,16,3,4,128]{4,3,2,1,0:T(4,128)(2,1)} reshape(bf16[2560,3,512]{2,1,0:T(4,128)(2,1)} %gather_fusion) | data formatting | bytes 15728640 | tf_op jit(solution)/shard_map/reshape | solution.py:36
  54.6 5.4 %fusion.17 = bf16[160,4,128]{2,1,0:T(4,128)(2,1)S(1)} fusion(bf16[160,16,3,4,128]{4,3,2,1,0:T(4,128)(2,1)} %reshape.205, pred[160,16]{1,0:T(8,128)(4,1)S(1)} %iota_compare_fusion.1), kind=kLoop, calls=%fused_computation.26 | loop fusion | flops 2539520 | bytes 2787840 | tf_op jit(solution)/shard_map/reduce_max | solution.py:38
  60.0 5.2 %slice_bitcast_fusion.2 = (bf16[160,16,4,128]{3,2,1,0:T(4,128)(2,1)S(1)}, bf16[160,16,4,128]{3,2,1,0:T(4,128)(2,1)S(1)}) fusion(bf16[160,16,3,4,128]{4,3,2,1,0:T(4,128)(2,1)} %reshape.205), kind=kLoop, calls=%fused_computation.22 | loop fusion | bytes 10485760 | tf_op jit(solution)/shard_map/squeeze | solution.py:49
  65.1 0.2 select_bitcast_fusion
  65.4 1.4 fusion.20
  66.8 0.2 copy.37
  67.1 0.2 copy.38
  67.3 0.8 fusion.18
  68.1 0.2 select_convert_fusion
  68.4 0.7 copy.80
  69.1 0.2 all-gather.5.cloned.1.call-start
  69.3 9.3 %copy.49 = bf16[512,8,2,512]{3,1,2,0:T(8,128)(2,1)} copy(bf16[512,8,2,512]{3,2,1,0:T(2,128)(2,1)} %bitcast.80) | data formatting | bytes 16777216
  78.6 44.9 %all-gather.3.cloned.1.call-done = bf16[160,4096]{1,0:T(8,128)(2,1)} async-done(((bf16[160,512]{1,0:T(8,128)(2,1)}), bf16[160,4096]{1,0:T(8,128)(2,1)}) %all-gather.3.cloned.1.call-update) | async-done | bytes 1310736 | tf_op jit(solution)/shard_map/all_gather | solution.py:58
  123.5 6.1 %convolution_convert_fusion = bf16[160,1024]{1,0:T(8,128)(2,1)} fusion(bf16[160,4096]{1,0:T(8,128)(2,1)} %all-gather.3.cloned.1.call-done, bf16[4096,1024]{1,0:T(8,128)(2,1)} %bitcast.81), kind=kOutput, calls=%fused_computation.32 | convolution fusion | flops 1342341120 | bytes 10027008 | tf_op jit(solution)/shard_map/dot_general | solution.py:57
  129.7 0.1 and.15
  129.8 0.6 fusion.15
  130.4 73.0 %all-gather.5.cloned.1.call-done = bf16[5120,1024]{1,0:T(8,128)(2,1)} async-done(((bf16[160,1024]{1,0:T(8,128)(2,1)}), bf16[5120,1024]{1,0:T(8,128)(2,1)}) %all-gather.5.cloned.1.call-update) | async-done | bytes 10485776 | tf_op jit(solution)/shard_map/all_gather | solution.py:66
  203.4 9.7 %slice_bitcast_fusion.1 = (bf16[640,4,8,128]{3,2,1,0:T(8,128)(2,1)}, bf16[640,4,8,128]{3,2,1,0:T(8,128)(2,1)}) fusion(bf16[5120,1024]{1,0:T(8,128)(2,1)} %all-gather.5.cloned.1.call-done), kind=kLoop, calls=%fused_computation.19 | loop fusion | bytes 20971520
  213.1 10.3 %fusion.2 = (f32[4,160]{1,0:T(4,128)S(1)}, f32[4,160,5120]{2,1,0:T(8,128)}) fusion(pred[160,5120]{1,0:T(8,128)(4,1)S(1)} %fusion.15, bf16[640,4,8,128]{3,2,1,0:T(8,128)(2,1)} %get-tuple-element.5, bf16[160,4,128]{2,1,0:T(4,128)(2,1)S(1)} %select_convert_fusion), kind=kOutput, calls=%fused_computation.5 | convolution fusion | flops 848690560 | bytes 19335680 | tf_op jit(solution)/shard_map/qhd,khd->hqk/dot_general | solution.py:74
  223.4 8.8 %fusion.3 = f32[4,160]{1,0:T(4,128)S(1)} fusion(f32[4,160,5120]{2,1,0:T(8,128)} %get-tuple-element.12, f32[4,160]{1,0:T(4,128)S(1)} %broadcast_maximum_fusion, pred[160,5120]{1,0:T(8,128)(4,1)S(1)} %fusion.15), kind=kLoop, calls=%fused_computation.6 | loop fusion | flops 16383360 | bytes 13931520 | tf_op jit(solution)/shard_map/reduce_sum | solution.py:80
  232.3 12.6 %fusion.33 = f32[4,20,8,128]{3,2,1,0:T(8,128)S(1)} fusion(bf16[640,4,8,128]{3,2,1,0:T(8,128)(2,1)} %get-tuple-element.6, f32[4,160,5120]{2,1,0:T(8,128)} %get-tuple-element.12, f32[4,160]{1,0:T(4,128)S(1)} %broadcast_maximum_fusion, pred[160,5120]{1,0:T(8,128)(4,1)S(1)} %fusion.15, f32[160,4]{0,1:T(4,128)S(1)} %compare_select_fusion.1), kind=kOutput, calls=%fused_computation.40 | convolution fusion | flops 5046353920 | bytes 19502080 | tf_op jit(solution)/shard_map/hqk,khd->hqd/dot_general | solution.py:81
  244.9 0.8 fusion.37
  (15 shorter events, 0.3 us)
Async XLA Ops:
  6.5 117.0 %all-gather.3.cloned.1.call-start = ((), (), s32[]{:S(2)}) async-start(), calls=%async_computation | async-start | bytes 1474560 | tf_op jit(solution)/shard_map/all_gather | solution.py:58
  9.3 1.4 copy-start
  10.7 6.4 %collective-permute-start = (bf16[16,3,512]{2,1,0:T(4,128)(2,1)S(1)}, bf16[16,3,512]{2,1,0:T(4,128)(2,1)S(1)}, u32[]{:S(2)}, u32[]{:S(2)}) collective-permute-start(bf16[16,3,512]{2,1,0:T(4,128)(2,1)S(1)} %slice.44), channel_id=1, source_target_pairs={{8,0},{16,8},{24,16},{32,24},{40,32},{48,40},{56,48},{64,56},{72,6... | collective-permute-start | bytes 147464 | tf_op jit(solution)/shard_map/ppermute | solution.py:16
  69.1 134.3 %all-gather.5.cloned.1.call-start = ((), (), s32[]{:S(2)}) async-start(), calls=%async_computation.1 | async-start | bytes 10813440 | tf_op jit(solution)/shard_map/all_gather | solution.py:66
  123.5 6.1 %copy-start.1 = (s32[32,161]{1,0:T(8,128)S(1)}, s32[32,161]{1,0:T(8,128)}, u32[]{:S(2)}) copy-start(s32[32,161]{1,0:T(8,128)} %param.5) | copy-start | bytes 61828
Sparse Core Ops, SparseCore 0:
  69.2 54.2 all-gather.2
  129.7 73.6 all-gather.4
where the time goes:
time: 253 us
  waiting for transfers between devices  118 us (47%)
  local copies, waits for them, and re-layouts  64.2 us (25%)
  matrix products  31.2 us (12%)
  other arithmetic  20.3 us (8%)
  between operations  13.6 us (5%)
  starting transfers between devices  5.33 us (2%)
    all_gather x1, waiting for transfers between devices, shards(): shard_piece = lax.all_gather(key_value, 'ctx', axis=0, tiled=True)  73 us
    all_gather x1, waiting for transfers between devices, shards(): lax.all_gather(patch_state, 'mp', axis=1, tiled=True)  44.9 us
    unnamed x8, local copies, waits for them, and re-layouts  23.8 us
    reshape x1, local copies, waits for them, and re-layouts, shards(): window = window.reshape(slot_count, WIN, 3, heads_here, head_dim)  21.7 us
    gather x1, local copies, waits for them, and re-layouts, shards(): window = extended[local_start[:, None] + offsets[None, :]]  12.8 us
    dot_general x1, matrix products, shards(): jnp.einsum('hqk,khd->hqd', exp_part, value_part.astype(jnp.float32), prec...  12.6 us
    dot_general x1, matrix products, shards(): jnp.einsum('qhd,khd->hqk', query_heads, key_part, preferred_element_type=...  10.3 us
    reduce_sum x1, other arithmetic, shards(): denom_sum = jnp.sum(exp_part, axis=2)  8.85 us
  transfers between devices with their start and end apart: 3, of which 3 were waited for; matrix products, arithmetic and copies ran while one was open for 4% of the time, Pallas kernels for 0%

commit v1 on v0

--- a/solution.py
+++ b/solution.py
@@ -55,7 +55,9 @@
     )
     flat_weight = kv_weight.reshape(kv_weight.shape[0], 2 * col_width)
     projected = jnp.dot(
-        lax.all_gather(patch_state, "mp", axis=1, tiled=True),
+        jnp.concatenate(
+            lax.all_to_all(jnp.stack([patch_state] * lax.axis_size("mp")), "mp", 0, 0), axis=1
+        ),
         flat_weight,
         preferred_element_type=jnp.float32,
     )

time: 253 us -> 226 us (0.89)
  waiting for transfers between devices: 118 us -> 83.4 us
  starting transfers between devices: 5.33 us -> 11.9 us
    all_gather x1 -> x0, waiting for transfers between devices: 44.9 us -> none  [shards(): lax.all_gather(patch_state, 'mp', axis=1, tiled=True)]
    all_to_all x0 -> x1, waiting for transfers between devices: none -> 9.75 us  [shards(): lax.all_to_all(jnp.stack([patch_state] * lax.axis_size('mp')), 'mp', 0, 0)]
    all_to_all x0 -> x1, starting transfers between devices: none -> 6.61 us  [shards(): lax.all_to_all(jnp.stack([patch_state] * lax.axis_size('mp')), 'mp', 0, 0)]
  transfers between devices with their start and end apart: 3 -> 3, of which waited for: 3 -> 3; matrix products, arithmetic and copies ran while one was open for 4% -> 5% of each run, Pallas kernels for 0% -> 0%
where the time goes in v1:
time: 226 us; the launch traced here: 225 us
  waiting for transfers between devices  83.4 us (37%)
  local copies, waits for them, and re-layouts  64.9 us (29%)
  matrix products  30.9 us (14%)
  other arithmetic  20.3 us (9%)
  between operations  13.6 us (6%)
  starting transfers between devices  11.9 us (5%)
    all_gather x1, waiting for transfers between devices, shards(): shard_piece = lax.all_gather(key_value, 'ctx', axis=0, tiled=True)  73.6 us
    unnamed x8, local copies, waits for them, and re-layouts  23.2 us
    reshape x1, local copies, waits for them, and re-layouts, shards(): window = window.reshape(slot_count, WIN, 3, heads_here, head_dim)  21.7 us
    gather x1, local copies, waits for them, and re-layouts, shards(): window = extended[local_start[:, None] + offsets[None, :]]  12.8 us
    dot_general x1, matrix products, shards(): jnp.einsum('hqk,khd->hqd', exp_part, value_part.astype(jnp.float32), prec...  12.6 us
    dot_general x1, matrix products, shards(): jnp.einsum('qhd,khd->hqk', query_heads, key_part, preferred_element_type=...  10.3 us
    all_to_all x1, waiting for transfers between devices, shards(): lax.all_to_all(jnp.stack([patch_state] * lax.axis_size('mp')), 'mp', 0, 0)  9.75 us
    reduce_sum x1, other arithmetic, shards(): denom_sum = jnp.sum(exp_part, axis=2)  8.85 us
  transfers between devices with their start and end apart: 3, of which 3 were waited for; matrix products, arithmetic and copies ran while one was open for 5% of the time, Pallas kernels for 0%

profile of v1, /device:TPU:1, one launch (start us, length us, event | category | flops | bytes accessed | tf_op | source)
XLA Modules:
  0.0 225.0 jit_solution(13234942373259320749)
XLA Ops:
  6.5 2.8 %copy.30 = bf16[512,3,512]{2,1,0:T(4,128)(2,1)S(1)} copy(bf16[512,3,512]{2,0,1:T(8,128)(2,1)} %param.3) | data formatting | bytes 3145728 | tf_op args[0]
  9.3 1.3 copy-done
  10.7 5.1 %collective-permute-start = (bf16[16,3,512]{2,1,0:T(4,128)(2,1)S(1)}, bf16[16,3,512]{2,1,0:T(4,128)(2,1)S(1)}, u32[]{:S(2)}, u32[]{:S(2)}) collective-permute-start(bf16[16,3,512]{2,1,0:T(4,128)(2,1)S(1)} %slice.44), channel_id=1, source_target_pairs={{8,0},{16,8},{24,16},{32,24},{40,32},{48,40},{56,48},{64,56},{72,6... | collective-permute-start | bytes 147464 | tf_op jit(solution)/shard_map/ppermute | solution.py:16
  15.8 0.9 dynamic-slice_subtract_fusion
  16.8 0.1 compare_select_fusion
  17.0 0.1 collective-permute-done
  17.1 3.0 %pad_maximum_fusion = bf16[528,3,512]{2,1,0:T(4,128)(2,1)S(1)} fusion(bf16[16,3,512]{2,1,0:T(4,128)(2,1)S(1)} %collective-permute-done, bf16[512,3,512]{2,1,0:T(4,128)(2,1)} %copy-done), kind=kLoop, calls=%fused_computation.31 | loop fusion | flops 811008 | bytes 3244032 | tf_op jit(solution)/shard_map/concatenate | solution.py:32
  20.1 12.8 %gather_fusion = bf16[2560,3,512]{2,1,0:T(4,128)(2,1)} fusion(bf16[528,3,512]{2,1,0:T(4,128)(2,1)S(1)} %pad_maximum_fusion, s32[3072]{0:T(1024)S(1)} %pad_clamp_fusion), kind=kCustom, calls=%fused_computation | custom fusion | bytes 15738880 | tf_op jit(solution)/shard_map/gather | solution.py:35
  33.0 21.7 %reshape.215 = bf16[160,16,3,4,128]{4,3,2,1,0:T(4,128)(2,1)} reshape(bf16[2560,3,512]{2,1,0:T(4,128)(2,1)} %gather_fusion) | data formatting | bytes 15728640 | tf_op jit(solution)/shard_map/reshape | solution.py:36
  54.6 5.4 %fusion.17 = bf16[160,4,128]{2,1,0:T(4,128)(2,1)S(1)} fusion(bf16[160,16,3,4,128]{4,3,2,1,0:T(4,128)(2,1)} %reshape.215, pred[160,16]{1,0:T(8,128)(4,1)S(1)} %iota_compare_fusion.1), kind=kLoop, calls=%fused_computation.26 | loop fusion | flops 2539520 | bytes 2787840 | tf_op jit(solution)/shard_map/reduce_max | solution.py:38
  60.0 5.2 %slice_bitcast_fusion.2 = (bf16[160,16,4,128]{3,2,1,0:T(4,128)(2,1)S(1)}, bf16[160,16,4,128]{3,2,1,0:T(4,128)(2,1)S(1)}) fusion(bf16[160,16,3,4,128]{4,3,2,1,0:T(4,128)(2,1)} %reshape.215), kind=kLoop, calls=%fused_computation.22 | loop fusion | bytes 10485760 | tf_op jit(solution)/shard_map/squeeze | solution.py:49
  65.1 0.2 select_bitcast_fusion
  65.4 1.4 fusion.20
  66.8 0.2 copy.39
  67.1 0.2 copy.40
  67.3 0.8 fusion.18
  68.1 0.2 select_convert_fusion
  68.4 1.3 stack.3
  69.7 6.6 %all-to-all-start = ((bf16[8,160,512]{2,1,0:T(8,128)(2,1)}), bf16[8,160,512]{2,1,0:T(8,128)(2,1)S(1)}, u32[]{:S(2)}, u32[]{:S(2)}) async-start(bf16[8,160,512]{2,1,0:T(8,128)(2,1)} %stack.3), calls=%async_computation | async-start | bytes 2621440 | tf_op jit(solution)/shard_map/all_to_all | solution.py:59
  76.3 0.2 all-gather.2.cloned.1.call-start
  76.5 9.3 %copy.52 = bf16[512,8,2,512]{3,1,2,0:T(8,128)(2,1)} copy(bf16[512,8,2,512]{3,2,1,0:T(2,128)(2,1)} %bitcast.83) | data formatting | bytes 16777216
  85.8 9.8 %all-to-all-done = bf16[8,160,512]{2,1,0:T(8,128)(2,1)S(1)} async-done(((bf16[8,160,512]{2,1,0:T(8,128)(2,1)}), bf16[8,160,512]{2,1,0:T(8,128)(2,1)S(1)}, u32[]{:S(2)}, u32[]{:S(2)}) %all-to-all-start) | async-done | bytes 1310752 | tf_op jit(solution)/shard_map/all_to_all | solution.py:59
  95.6 0.1 copy.49
  95.7 5.7 %convolution_convert_fusion = bf16[160,1024]{1,0:T(8,128)(2,1)} fusion(bf16[160,4096]{1,0:T(8,128)(2,1)S(1)} %bitcast.88, bf16[4096,1024]{1,0:T(8,128)(2,1)} %bitcast.84), kind=kOutput, calls=%fused_computation.32 | convolution fusion | flops 1342341120 | bytes 10027008 | tf_op jit(solution)/shard_map/dot_general | solution.py:57
  101.5 0.1 and.15
  101.7 0.6 fusion.15
  102.3 73.6 %all-gather.2.cloned.1.call-done = bf16[5120,1024]{1,0:T(8,128)(2,1)} async-done(((bf16[160,1024]{1,0:T(8,128)(2,1)}), bf16[5120,1024]{1,0:T(8,128)(2,1)}) %all-gather.2.cloned.1.call-update) | async-done | bytes 10485776 | tf_op jit(solution)/shard_map/all_gather | solution.py:68
  175.8 9.7 %slice_bitcast_fusion.1 = (bf16[640,4,8,128]{3,2,1,0:T(8,128)(2,1)}, bf16[640,4,8,128]{3,2,1,0:T(8,128)(2,1)}) fusion(bf16[5120,1024]{1,0:T(8,128)(2,1)} %all-gather.2.cloned.1.call-done), kind=kLoop, calls=%fused_computation.19 | loop fusion | bytes 20971520
  185.6 10.3 %fusion.2 = (f32[4,160]{1,0:T(4,128)S(1)}, f32[4,160,5120]{2,1,0:T(8,128)}) fusion(pred[160,5120]{1,0:T(8,128)(4,1)S(1)} %fusion.15, bf16[640,4,8,128]{3,2,1,0:T(8,128)(2,1)} %get-tuple-element.5, bf16[160,4,128]{2,1,0:T(4,128)(2,1)S(1)} %select_convert_fusion), kind=kOutput, calls=%fused_computation.5 | convolution fusion | flops 848690560 | bytes 19335680 | tf_op jit(solution)/shard_map/qhd,khd->hqk/dot_general | solution.py:76
  195.9 8.8 %fusion.3 = f32[4,160]{1,0:T(4,128)S(1)} fusion(f32[4,160,5120]{2,1,0:T(8,128)} %get-tuple-element.12, f32[4,160]{1,0:T(4,128)S(1)} %broadcast_maximum_fusion, pred[160,5120]{1,0:T(8,128)(4,1)S(1)} %fusion.15), kind=kLoop, calls=%fused_computation.6 | loop fusion | flops 16383360 | bytes 13931520 | tf_op jit(solution)/shard_map/reduce_sum | solution.py:82
  204.7 12.6 %fusion.33 = f32[4,20,8,128]{3,2,1,0:T(8,128)S(1)} fusion(bf16[640,4,8,128]{3,2,1,0:T(8,128)(2,1)} %get-tuple-element.6, f32[4,160,5120]{2,1,0:T(8,128)} %get-tuple-element.12, f32[4,160]{1,0:T(4,128)S(1)} %broadcast_maximum_fusion, pred[160,5120]{1,0:T(8,128)(4,1)S(1)} %fusion.15, f32[160,4]{0,1:T(4,128)S(1)} %compare_select_fusion.1), kind=kOutput, calls=%fused_computation.40 | convolution fusion | flops 5046353920 | bytes 19502080 | tf_op jit(solution)/shard_map/hqk,khd->hqd/dot_general | solution.py:83
  217.4 0.8 fusion.37
  (16 shorter events, 0.5 us)
Async XLA Ops:
  9.3 1.4 copy-start
  10.7 6.4 %collective-permute-start = (bf16[16,3,512]{2,1,0:T(4,128)(2,1)S(1)}, bf16[16,3,512]{2,1,0:T(4,128)(2,1)S(1)}, u32[]{:S(2)}, u32[]{:S(2)}) collective-permute-start(bf16[16,3,512]{2,1,0:T(4,128)(2,1)S(1)} %slice.44), channel_id=1, source_target_pairs={{8,0},{16,8},{24,16},{32,24},{40,32},{48,40},{56,48},{64,56},{72,6... | collective-permute-start | bytes 147464 | tf_op jit(solution)/shard_map/ppermute | solution.py:16
  69.7 25.9 %all-to-all-start = ((bf16[8,160,512]{2,1,0:T(8,128)(2,1)}), bf16[8,160,512]{2,1,0:T(8,128)(2,1)S(1)}, u32[]{:S(2)}, u32[]{:S(2)}) async-start(bf16[8,160,512]{2,1,0:T(8,128)(2,1)} %stack.3), calls=%async_computation | async-start | bytes 2621440 | tf_op jit(solution)/shard_map/all_to_all | solution.py:59
  76.3 99.6 %all-gather.2.cloned.1.call-start = ((), (), s32[]{:S(2)}) async-start(), calls=%async_computation.1 | async-start | bytes 10813440 | tf_op jit(solution)/shard_map/all_gather | solution.py:68
  95.7 5.7 %copy-start.1 = (s32[32,161]{1,0:T(8,128)S(1)}, s32[32,161]{1,0:T(8,128)}, u32[]{:S(2)}) copy-start(s32[32,161]{1,0:T(8,128)} %param.5) | copy-start | bytes 61828
Sparse Core Ops, SparseCore 0:
  101.6 74.2 all-gather.1
